TPU v7x, 256 devices: a whole 4x4x8 slice. The times are simulated.
256 devices in a mesh: tm: 128 (over z, y, x), rhs: 2 (over core).
Axes of the slice: x: 4, y: 4, z: 8, core: 2. Of those that a mesh axis runs over, the one named last changes fastest.
Arguments:
- diag: float32 [262144, 512], P('tm', 'rhs'), as said below
- lower: float32 [262144, 512], P('tm', 'rhs'), as said below
- right_side: float32 [128, 262144], P('rhs', 'tm'), may hold values from -6 to 6
- coarse_sol: float32 [128, 65536], P('rhs', 'tm'), may hold values from -6 to 6
Outputs:
- coarse_diag: float32 [65536, 512], P('tm', 'rhs')
- coarse_lower: float32 [65536, 512], P('tm', 'rhs')
- coarse_rhs: float32 [128, 65536], P('rhs', 'tm')
- solution: float32 [128, 262144], P('rhs', 'tm')
Inputs may be any that keep to these rules, and one draw needn't show every extreme that they name: diag and lower are the diagonal and coupling blocks of a symmetric positive definite periodic block tridiagonal matrix whose eigenvalues are all at least 2; every diagonal block is symmetric. lower holds the coupling blocks of the matrix described for diag.
All inputs are finite; a program needn't handle non-finite values.
Results may differ from a plain program's by a relative error of at most 0.0003.
Values sent between devices are 32-bit elements; how exact they have to be, the bound alone decides.
A program may use at most 128 MiB of HBM per device.

v0:
```python
import jax
import jax.numpy as jnp
from jax import lax
from jax.sharding import PartitionSpec as P


def shifted(shard, axis, by):
    size = lax.axis_size(axis)
    return lax.ppermute(shard, axis, [(i, (i + by) % size) for i in range(size)])


def product(first_term, second_term):
    return jnp.dot(
        first_term, second_term, precision=lax.Precision.HIGHEST, preferred_element_type=jnp.float32
    )


def apply_inverse(factor, stacked):
    halfway = lax.linalg.triangular_solve(factor, stacked, left_side=True, lower=True)
    return lax.linalg.triangular_solve(
        factor, halfway, left_side=True, lower=True, transpose_a=True
    )


def slice_cols(matrix, first_col, col_count):
    return lax.dynamic_slice_in_dim(matrix, first_col, col_count, 1)


def slice_rows(matrix, first_row, row_count):
    return lax.dynamic_slice_in_dim(matrix, first_row, row_count, 0)


def eliminate_one(diag_block, link_block, next_link, rhs_block, first_col, col_count):
    factor = jnp.linalg.cholesky(diag_block)
    stacked = jnp.concatenate(
        [
            slice_cols(link_block, first_col, col_count),
            slice_rows(next_link, first_col, col_count).T,
            rhs_block,
        ],
        axis=1,
    )
    solved = apply_inverse(factor, stacked)
    return (
        factor,
        solved[:, :col_count],
        solved[:, col_count : 2 * col_count],
        solved[:, 2 * col_count :],
    )


def shards(diag, lower, right_side, coarse_sol):
    span_cols = diag.shape[1]
    block_order = span_cols * lax.axis_size("rhs")
    column_start = lax.axis_index("rhs") * span_cols
    next_share = shifted(lower[:block_order], "tm", -1)
    full_diag, full_lower, next_lower = (
        lax.all_gather(diag, "rhs", axis=1, tiled=True),
        lax.all_gather(lower, "rhs", axis=1, tiled=True),
        lax.all_gather(next_share, "rhs", axis=1, tiled=True),
    )
    diag_blocks = [
        full_diag[position * block_order : (position + 1) * block_order] for position in range(4)
    ]
    link_blocks = [
        full_lower[position * block_order : (position + 1) * block_order] for position in range(4)
    ]
    rhs_blocks = [
        right_side[:, position * block_order : (position + 1) * block_order].T
        for position in range(4)
    ]
    factor_one, prev_one, next_one, own_one = eliminate_one(
        diag_blocks[1], link_blocks[1], link_blocks[2], rhs_blocks[1], column_start, span_cols
    )
    factor_three, prev_three, next_three, own_three = eliminate_one(
        diag_blocks[3], link_blocks[3], next_lower, rhs_blocks[3], column_start, span_cols
    )
    came_prev, came_next, came_own = shifted((prev_three, next_three, own_three), "tm", 1)
    kept_diag = (
        slice_cols(diag_blocks[0], column_start, span_cols)
        - product(link_blocks[1].T, prev_one)
        - product(link_blocks[0], came_next)
    )
    kept_link = -product(link_blocks[0], came_prev)
    kept_rhs = (
        rhs_blocks[0] - product(link_blocks[1].T, own_one) - product(link_blocks[0], came_own)
    )
    odd_diag = (
        slice_cols(diag_blocks[2], column_start, span_cols)
        - product(link_blocks[3].T, prev_three)
        - product(link_blocks[2], next_one)
    )
    odd_link = -product(link_blocks[2], prev_one)
    odd_rhs = (
        rhs_blocks[2] - product(link_blocks[3].T, own_three) - product(link_blocks[2], own_one)
    )
    next_piece = shifted(kept_link, "tm", -1)
    odd_full, kept_link_full, odd_link_full, following = (
        lax.all_gather(odd_diag, "rhs", axis=1, tiled=True),
        lax.all_gather(kept_link, "rhs", axis=1, tiled=True),
        lax.all_gather(odd_link, "rhs", axis=1, tiled=True),
        lax.all_gather(next_piece, "rhs", axis=1, tiled=True),
    )
    factor_odd, prev_two, next_two, own_two = eliminate_one(
        odd_full, odd_link_full, following, odd_rhs, column_start, span_cols
    )
    came_prev_two, came_next_two, came_own_two = shifted((prev_two, next_two, own_two), "tm", 1)
    coarse_diag = (
        kept_diag - product(odd_link_full.T, prev_two) - product(kept_link_full, came_next_two)
    )
    coarse_lower = -product(kept_link_full, came_prev_two)
    coarse_rhs = (
        kept_rhs - product(odd_link_full.T, own_two) - product(kept_link_full, came_own_two)
    )
    kept_values = coarse_sol.T
    later_values = shifted(coarse_sol, "tm", -1).T
    odd_values = apply_inverse(
        factor_odd,
        odd_rhs - product(odd_link_full, kept_values) - product(following.T, later_values),
    )
    first_values = apply_inverse(
        factor_one,
        rhs_blocks[1]
        - product(link_blocks[1], kept_values)
        - product(link_blocks[2].T, odd_values),
    )
    third_values = apply_inverse(
        factor_three,
        rhs_blocks[3] - product(link_blocks[3], odd_values) - product(next_lower.T, later_values),
    )
    solution = jnp.concatenate([kept_values, first_values, odd_values, third_values], axis=0).T
    return (coarse_diag, coarse_lower, coarse_rhs.T, solution)


def solution(mesh):
    return jax.shard_map(
        shards,
        mesh=mesh,
        in_specs=(P("tm", "rhs"), P("tm", "rhs"), P("rhs", "tm"), P("rhs", "tm")),
        out_specs=(P("tm", "rhs"), P("tm", "rhs"), P("rhs", "tm"), P("rhs", "tm")),
        check_vma=False,
    )
```

profile of v0, /device:TPU:0, one launch (start us, length us, event | category | flops | bytes accessed | tf_op | source)
XLA Modules:
  0.0 676.5 jit_solution(9035725231035911094)
XLA Ops:
  17.2 11.2 %collective-permute-done = f32[512,256]{1,0:T(8,128)S(1)} collective-permute-done((f32[512,256]{1,0:T(8,128)S(1)}, f32[512,256]{1,0:T(8,128)S(1)}, u32[]{:S(2)}, u32[]{:S(2)}) %collective-permute-start) | collective-permute-done | bytes 524320 | tf_op jit(solution)/shard_map/ppermute | solution.py:9
  44.5 20.3 %all-gather.8.cloned.1.call-done = f32[2048,512]{0,1:T(8,128)} async-done(((f32[2048,256]{0,1:T(8,128)}), f32[2048,512]{0,1:T(8,128)}) %all-gather.8.cloned.1.call-update) | async-done | bytes 4194320 | tf_op jit(solution)/shard_map/all_gather | solution.py:58
  72.6 11.7 %cholesky.374 = f32[128,128]{1,0:T(8,128)S(1)} custom-call(f32[128,128]{1,0:T(8,128)S(1)} %cholesky.586), custom_call_target="Cholesky" | custom-call | tf_op jit(solution)/shard_map/jit(cholesky)/cholesky | solution.py:34
  95.0 11.9 %cholesky.393 = f32[128,128]{1,0:T(8,128)S(1)} custom-call(f32[128,128]{1,0:T(8,128)S(1)} %cholesky.590), custom_call_target="Cholesky" | custom-call | tf_op jit(solution)/shard_map/jit(cholesky)/cholesky | solution.py:34
  106.9 9.8 %custom-call.47 = f32[1,128,128]{1,2,0:T(8,128)S(1)} custom-call(f32[1,128,128]{2,1,0:T(8,128)S(1)} %get-tuple-element.176), custom_call_target="InvertDiagBlocksLowerTriangular" | custom-call | tf_op jit(solution)/shard_map/jit(cholesky)/cholesky | solution.py:34
  117.4 11.7 %cholesky.414 = f32[128,128]{1,0:T(8,128)S(1)} custom-call(f32[128,128]{1,0:T(8,128)S(1)} %cholesky.595), custom_call_target="Cholesky" | custom-call | tf_op jit(solution)/shard_map/jit(cholesky)/cholesky | solution.py:34
  139.6 22.7 %cholesky.431 = f32[128,128]{1,0:T(8,128)S(1)} custom-call(f32[128,128]{1,0:T(8,128)S(1)} %convolution_subtract_fusion.30), custom_call_target="Cholesky" | custom-call | tf_op jit(solution)/shard_map/jit(cholesky)/cholesky | solution.py:34
  175.2 39.3 %custom-call.50 = f32[4,128,128]{1,2,0:T(8,128)S(1)} custom-call(f32[4,128,128]{2,1,0:T(8,128)S(1)} %get-tuple-element.90), custom_call_target="InvertDiagBlocksLowerTriangular" | custom-call | tf_op jit(solution)/shard_map/triangular_solve/custom-call.8 | solution.py:20
  229.2 12.1 %cholesky.446 = f32[128,128]{1,0:T(8,128)S(1)} custom-call(f32[128,128]{1,0:T(8,128)S(1)} %cholesky.599), custom_call_target="Cholesky" | custom-call | tf_op jit(solution)/shard_map/jit(cholesky)/cholesky | solution.py:34
  253.8 11.7 %cholesky.465 = f32[128,128]{1,0:T(8,128)S(1)} custom-call(f32[128,128]{1,0:T(8,128)S(1)} %cholesky.603), custom_call_target="Cholesky" | custom-call | tf_op jit(solution)/shard_map/jit(cholesky)/cholesky | solution.py:34
  276.9 11.9 %cholesky.486 = f32[128,128]{1,0:T(8,128)S(1)} custom-call(f32[128,128]{1,0:T(8,128)S(1)} %cholesky.608), custom_call_target="Cholesky" | custom-call | tf_op jit(solution)/shard_map/jit(cholesky)/cholesky | solution.py:34
  300.7 11.7 %cholesky.503 = f32[128,128]{1,0:T(8,128)S(1)} custom-call(f32[128,128]{1,0:T(8,128)S(1)} %convolution_subtract_fusion.29), custom_call_target="Cholesky" | custom-call | tf_op jit(solution)/shard_map/jit(cholesky)/cholesky | solution.py:34
  326.5 40.5 %custom-call.55 = f32[4,128,128]{1,2,0:T(8,128)S(1)} custom-call(f32[4,128,128]{2,1,0:T(8,128)} %copy-done.45), custom_call_target="InvertDiagBlocksLowerTriangular" | custom-call | tf_op jit(solution)/shard_map/triangular_solve/custom-call.8 | solution.py:20
  389.6 15.5 %collective-permute-done.2 = f32[512,256]{0,1:T(8,128)} collective-permute-done((f32[512,256]{0,1:T(8,128)}, f32[512,256]{0,1:T(8,128)}, u32[]{:S(2)}, u32[]{:S(2)}) %collective-permute-start.2) | collective-permute-done | bytes 524320 | tf_op jit(solution)/shard_map/ppermute | solution.py:9
  440.8 11.7 %cholesky.518 = f32[128,128]{1,0:T(8,128)S(1)} custom-call(f32[128,128]{1,0:T(8,128)S(1)} %cholesky.612), custom_call_target="Cholesky" | custom-call | tf_op jit(solution)/shard_map/jit(cholesky)/cholesky | solution.py:34
  454.8 11.3 %custom-call.56 = f32[1,128,128]{1,2,0:T(8,128)} custom-call(f32[1,128,128]{2,1,0:T(8,128)} %get-tuple-element.159), custom_call_target="InvertDiagBlocksLowerTriangular" | custom-call | tf_op jit(solution)/shard_map/jit(cholesky)/cholesky | solution.py:34
  469.9 13.6 %cholesky.537 = f32[128,128]{1,0:T(8,128)} custom-call(f32[128,128]{1,0:T(8,128)} %cholesky.616), custom_call_target="Cholesky" | custom-call | tf_op jit(solution)/shard_map/jit(cholesky)/cholesky | solution.py:34
  486.3 11.3 %custom-call.57 = f32[1,128,128]{1,2,0:T(8,128)} custom-call(f32[1,128,128]{2,1,0:T(8,128)} %get-tuple-element.156), custom_call_target="InvertDiagBlocksLowerTriangular" | custom-call | tf_op jit(solution)/shard_map/jit(cholesky)/cholesky | solution.py:34
  501.3 13.2 %cholesky.558 = f32[128,128]{1,0:T(8,128)} custom-call(f32[128,128]{1,0:T(8,128)} %cholesky.621), custom_call_target="Cholesky" | custom-call | tf_op jit(solution)/shard_map/jit(cholesky)/cholesky | solution.py:34
  516.6 11.3 %custom-call.58 = f32[1,128,128]{1,2,0:T(8,128)} custom-call(f32[1,128,128]{2,1,0:T(8,128)} %get-tuple-element.153), custom_call_target="InvertDiagBlocksLowerTriangular" | custom-call | tf_op jit(solution)/shard_map/jit(cholesky)/cholesky | solution.py:34
  530.8 13.3 %cholesky.575 = f32[128,128]{1,0:T(8,128)} custom-call(f32[128,128]{1,0:T(8,128)} %convolution_subtract_fusion.28), custom_call_target="Cholesky" | custom-call | tf_op jit(solution)/shard_map/jit(cholesky)/cholesky | solution.py:34
  550.5 10.2 %while.26 = (s32[]{:T(128)}, f32[512,512]{1,0:T(8,128)S(1)}, s32[4,2]{0,1:T(2,128)S(1)}, f32[4,128,128]{2,1,0:T(8,128)}, s32[]{:T(128)}) while((s32[]{:T(128)}, f32[512,512]{1,0:T(8,128)S(1)}, s32[4,2]{0,1:T(2,128)S(1)}, f32[4,128,128]{2,1,0:T(8,128)}, s32[]{:T(128)}) %tuple.144), condition=%wide.while_cond.1.clone.1, body=%wide.while_body.1.clone.1.sunk | while | flops 2 | bytes 132705 | solution.py:20
  560.7 40.8 %custom-call.60 = f32[4,128,128]{1,2,0:T(8,128)} custom-call(f32[4,128,128]{2,1,0:T(8,128)} %get-tuple-element.94), custom_call_target="InvertDiagBlocksLowerTriangular" | custom-call | tf_op jit(solution)/shard_map/triangular_solve/custom-call.8 | solution.py:20
  647.5 15.8 %collective-permute-done.4 = f32[512,256]{0,1:T(8,128)} collective-permute-done((f32[512,256]{0,1:T(8,128)S(1)}, f32[512,256]{0,1:T(8,128)}, u32[]{:S(2)}, u32[]{:S(2)}) %collective-permute-start.4) | collective-permute-done | bytes 524320 | tf_op jit(solution)/shard_map/ppermute | solution.py:9
  (367 shorter events, 284.5 us)
Async XLA Ops:
  7.2 35.5 %all-gather.12.cloned.1.call-start = ((), (), s32[]{:S(2)}) async-start(), calls=%async_computation.2 | async-start | bytes 1572864 | tf_op jit(solution)/shard_map/all_gather | solution.py:60
  8.3 20.1 %collective-permute-start = (f32[512,256]{1,0:T(8,128)S(1)}, f32[512,256]{1,0:T(8,128)S(1)}, u32[]{:S(2)}, u32[]{:S(2)}) collective-permute-start(f32[512,256]{1,0:T(8,128)S(1)} %slice.264), channel_id=1, source_target_pairs={{0,254},{2,0},{4,2},{6,4},{8,6},{10,8},{12,10},{14,12},{16,14},{18... | collective-permute-start | bytes 1572872 | tf_op jit(solution)/shard_map/ppermute | solution.py:9
  29.2 35.6 %all-gather.8.cloned.1.call-start = ((), (), s32[]{:S(2)}) async-start(), calls=%async_computation | async-start | bytes 6291456 | tf_op jit(solution)/shard_map/all_gather | solution.py:58
  32.2 182.4 %all-gather.10.cloned.1.call-start = ((), (), s32[]{:S(2)}) async-start(), calls=%async_computation.1 | async-start | bytes 6291456 | tf_op jit(solution)/shard_map/all_gather | solution.py:59
  35.6 399.9 %all-gather.16.cloned.1.call-start = ((), (), s32[]{:S(2)}) async-start(), calls=%async_computation.4 | async-start | bytes 1572864 | tf_op jit(solution)/shard_map/all_gather | solution.py:99
  317.7 50.5 %copy-start.39 = (f32[512,64]{0,1:T(8,128)S(1)}, f32[512,64]{0,1:T(8,128)}, u32[]{:S(2)}) copy-start(f32[512,64]{0,1:T(8,128)} %get-tuple-element.148) | copy-start | bytes 393220
  382.8 218.7 %all-gather.14.cloned.1.call-start = ((), (), s32[]{:S(2)}) async-start(), calls=%async_computation.3 | async-start | bytes 1572864 | tf_op jit(solution)/shard_map/all_gather | solution.py:101
  385.1 20.0 %collective-permute-start.2 = (f32[512,256]{0,1:T(8,128)}, f32[512,256]{0,1:T(8,128)}, u32[]{:S(2)}, u32[]{:S(2)}) collective-permute-start(f32[512,256]{0,1:T(8,128)} %get-tuple-element.147), channel_id=1, source_target_pairs={{0,2},{2,4},{4,6},{6,8},{8,10},{10,12},{12,14},{14,16},{16,18},{18... | collective-permute-start | bytes 1572872 | tf_op jit(solution)/shard_map/ppermute | solution.py:9
  389.5 216.3 %all-gather.18.cloned.1.call-start = ((), (), s32[]{:S(2)}) async-start(), calls=%async_computation.5 | async-start | bytes 1572864 | tf_op jit(solution)/shard_map/all_gather | solution.py:102
  409.1 5.5 copy-start.12
  409.1 5.5 copy-start.22
  409.1 15.1 %collective-permute-start.3 = (f32[512,256]{1,0:T(8,128)}, f32[512,256]{1,0:T(8,128)}, u32[]{:S(2)}, u32[]{:S(2)}) collective-permute-start(f32[512,256]{1,0:T(8,128)} %fusion), channel_id=1, source_target_pairs={{0,254},{2,0},{4,2},{6,4},{8,6},{10,8},{12,10},{14,12},{16,14},{18... | collective-permute-start | bytes 1572872 | tf_op jit(solution)/shard_map/ppermute | solution.py:9
  410.8 205.0 %collective-permute-start.8 = (f32[64,512]{1,0:T(8,128)}, f32[64,512]{1,0:T(8,128)}, u32[]{:S(2)}, u32[]{:S(2)}) collective-permute-start(f32[64,512]{1,0:T(8,128)} %param.16), channel_id=1, source_target_pairs={{0,254},{2,0},{4,2},{6,4},{8,6},{10,8},{12,10},{14,12},{16,14},{18... | collective-permute-start | bytes 393224 | tf_op jit(solution)/shard_map/ppermute | solution.py:9
  413.1 222.5 %collective-permute-start.6 = (f32[512,64]{0,1:T(8,128)}, f32[512,64]{0,1:T(8,128)}, u32[]{:S(2)}, u32[]{:S(2)}) collective-permute-start(f32[512,64]{0,1:T(8,128)} %pad_maximum_fusion.8), channel_id=1, source_target_pairs={{0,2},{2,4},{4,6},{6,8},{8,10},{10,12},{12,14},{14,16},{16,18},{18... | collective-permute-start | bytes 393224 | tf_op jit(solution)/shard_map/ppermute | solution.py:9
  414.3 225.3 %collective-permute-start.1 = (f32[512,256]{0,1:T(8,128)}, f32[512,256]{0,1:T(8,128)}, u32[]{:S(2)}, u32[]{:S(2)}) collective-permute-start(f32[512,256]{0,1:T(8,128)} %get-tuple-element.146), channel_id=1, source_target_pairs={{0,2},{2,4},{4,6},{6,8},{8,10},{10,12},{12,14},{14,16},{16,18},{18... | collective-permute-start | bytes 1572872 | tf_op jit(solution)/shard_map/ppermute | solution.py:9
  414.6 9.9 %copy-start.32 = (f32[64,2048]{1,0:T(8,128)S(1)}, f32[64,2048]{1,0:T(8,128)}, u32[]{:S(2)}) copy-start(f32[64,2048]{1,0:T(8,128)} %param.15) | copy-start | bytes 1572868
  414.6 9.9 %copy-start.33 = (f32[64,512]{1,0:T(8,128)S(1)}, f32[64,512]{1,0:T(8,128)}, u32[]{:S(2)}) copy-start(f32[64,512]{1,0:T(8,128)} %param.16) | copy-start | bytes 393220
  424.2 218.6 %all-gather.20.cloned.1.call-start = ((), (), s32[]{:S(2)}) async-start(), calls=%async_computation.6 | async-start | bytes 1572864 | tf_op jit(solution)/shard_map/all_gather | solution.py:100
  560.7 40.8 %copy-start.4 = (f32[512,512]{1,0:T(8,128)}, f32[512,512]{1,0:T(8,128)S(1)}, u32[]{:S(2)}) copy-start(f32[512,512]{1,0:T(8,128)S(1)} %get-tuple-element.339) | copy-start | bytes 3145732
  615.7 5.9 copy-start.1
  632.2 12.2 %collective-permute-start.7 = (f32[512,64]{0,1:T(8,128)}, f32[512,64]{0,1:T(8,128)}, u32[]{:S(2)}, u32[]{:S(2)}) collective-permute-start(f32[512,64]{0,1:T(8,128)} %pad_maximum_fusion.6), channel_id=1, source_target_pairs={{0,2},{2,4},{4,6},{6,8},{8,10},{10,12},{12,14},{14,16},{16,18},{18... | collective-permute-start | bytes 393224 | tf_op jit(solution)/shard_map/ppermute | solution.py:9
  633.2 33.3 %collective-permute-start.5 = (f32[512,256]{0,1:T(8,128)}, f32[512,256]{0,1:T(8,128)}, u32[]{:S(2)}, u32[]{:S(2)}) collective-permute-start(f32[512,256]{0,1:T(8,128)} %get-tuple-element.144), channel_id=1, source_target_pairs={{0,2},{2,4},{4,6},{6,8},{8,10},{10,12},{12,14},{14,16},{16,18},{18... | collective-permute-start | bytes 1572872 | tf_op jit(solution)/shard_map/ppermute | solution.py:9
  633.2 30.1 %collective-permute-start.4 = (f32[512,256]{0,1:T(8,128)S(1)}, f32[512,256]{0,1:T(8,128)}, u32[]{:S(2)}, u32[]{:S(2)}) collective-permute-start(f32[512,256]{0,1:T(8,128)S(1)} %get-tuple-element.145), channel_id=1, source_target_pairs={{0,2},{2,4},{4,6},{6,8},{8,10},{10,12},{12,14},{14,16},{16,18},{18... | collective-permute-start | bytes 1572872 | tf_op jit(solution)/shard_map/ppermute | solution.py:9
  642.9 20.4 %copy-start.3 = (f32[512,512]{1,0:T(8,128)S(1)}, f32[512,512]{1,0:T(8,128)}, u32[]{:S(2)}) copy-start(f32[512,512]{1,0:T(8,128)} %all-gather.20.cloned.1.call-done) | copy-start | bytes 3145732
  (38 other events, 76.9 us)
Sparse Core Ops, SparseCore 0:
  29.3 13.3 all-gather.11
  44.5 20.2 all-gather.7
  66.6 20.4 all-gather.9
  382.9 15.6 all-gather.15
  400.8 15.6 all-gather.13
  424.3 13.5 all-gather.17
  440.3 15.7 all-gather.19
where the time goes:
time: 688 us; the launch traced here: 676 us
  other arithmetic  393 us (57%)
  matrix products  97.5 us (14%)
  waiting for transfers between devices  76 us (11%)
  local copies, waits for them, and re-layouts  71.3 us (10%)
  between operations  23.6 us (3%)
  starting transfers between devices  14.9 us (2%)
    another operation x43, other arithmetic, eliminate_one(): factor = jnp.linalg.cholesky(diag_block)  262 us
    another operation x10, other arithmetic, apply_inverse(): lax.linalg.triangular_solve(factor, halfway, left_side=True, lower=True,...  124 us
    ppermute x9, waiting for transfers between devices, shifted(): lax.ppermute(shard, axis, [(i, (i + by) % size) for i in range(size)])  51.1 us
    dot_general x21, matrix products, product(): jnp.dot(first_term, second_term, precision=lax.Precision.HIGHEST, preferr...  48.1 us
    another operation x40, local copies, waits for them, and re-layouts, apply_inverse(): lax.linalg.triangular_solve(factor, halfway, left_side=True, lower=True,...  26.8 us
    all_gather x1, waiting for transfers between devices, shards(): lax.all_gather(diag, 'rhs', axis=1, tiled=True)  20.3 us
    unnamed x96, local copies, waits for them, and re-layouts  18.5 us
    another operation x42, matrix products, apply_inverse(): lax.linalg.triangular_solve(factor, halfway, left_side=True, lower=True,...  17.2 us
  transfers between devices with their start and end apart: 16, of which 7 were waited for; matrix products, arithmetic and copies ran while one was open for 57% of the time, Pallas kernels for 0%

commit v1 on v0

--- a/solution.py
+++ b/solution.py
@@ -2,6 +2,7 @@
 import jax.numpy as jnp
 from jax import lax
 from jax.sharding import PartitionSpec as P
+from jax.lax import all_to_all, psum
 
 
 def shifted(shard, axis, by):
@@ -54,8 +55,11 @@
     block_order = span_cols * lax.axis_size("rhs")
     column_start = lax.axis_index("rhs") * span_cols
     next_share = shifted(lower[:block_order], "tm", -1)
+    lane_do = lambda frame: jnp.concatenate(
+        all_to_all(jnp.stack([frame for _ in range(psum(1, "rhs"))], axis=0), "rhs", 0, 0), axis=1
+    )
     full_diag, full_lower, next_lower = (
-        lax.all_gather(diag, "rhs", axis=1, tiled=True),
+        lane_do(diag),
         lax.all_gather(lower, "rhs", axis=1, tiled=True),
         lax.all_gather(next_share, "rhs", axis=1, tiled=True),
     )

time: 688 us -> 667 us (0.969)
  waiting for transfers between devices: 76 us -> 52.4 us
    all_gather x1 -> x0, waiting for transfers between devices: 20.3 us -> none  [shards(): lax.all_gather(diag, 'rhs', axis=1, tiled=True)]
    unnamed x96 -> x103, local copies, waits for them, and re-layouts: 18.5 us -> 15.2 us
  transfers between devices with their start and end apart: 16 -> 16, of which waited for: 7 -> 6; matrix products, arithmetic and copies ran while one was open for 57% -> 79% of each run, Pallas kernels for 0% -> 0%
where the time goes in v1:
time: 667 us; the launch traced here: 654 us
  other arithmetic  389 us (58%)
  matrix products  95.4 us (14%)
  local copies, waits for them, and re-layouts  74.5 us (11%)
  waiting for transfers between devices  52.4 us (8%)
  between operations  23.8 us (4%)
  starting transfers between devices  19.2 us (3%)
    another operation x43, other arithmetic, eliminate_one(): factor = jnp.linalg.cholesky(diag_block)  255 us
    another operation x10, other arithmetic, apply_inverse(): lax.linalg.triangular_solve(factor, halfway, left_side=True, lower=True,...  123 us
    ppermute x9, waiting for transfers between devices, shifted(): lax.ppermute(shard, axis, [(i, (i + by) % size) for i in range(size)])  50.7 us
    dot_general x21, matrix products, product(): jnp.dot(first_term, second_term, precision=lax.Precision.HIGHEST, preferr...  48 us
    another operation x40, local copies, waits for them, and re-layouts, apply_inverse(): lax.linalg.triangular_solve(factor, halfway, left_side=True, lower=True,...  27 us
    another operation x42, matrix products, apply_inverse(): lax.linalg.triangular_solve(factor, stacked, left_side=True, lower=True)  17.4 us
    another operation x42, matrix products, apply_inverse(): lax.linalg.triangular_solve(factor, halfway, left_side=True, lower=True,...  16.6 us
    unnamed x103, local copies, waits for them, and re-layouts  15.2 us
  transfers between devices with their start and end apart: 16, of which 6 were waited for; matrix products, arithmetic and copies ran while one was open for 79% of the time, Pallas kernels for 0%

profile of v1, /device:TPU:0, one launch (start us, length us, event | category | flops | bytes accessed | tf_op | source)
XLA Modules:
  0.0 654.3 jit_solution(13338508129184685755)
XLA Ops:
  17.2 11.2 %collective-permute-done = f32[512,256]{1,0:T(8,128)S(1)} collective-permute-done((f32[512,256]{1,0:T(8,128)S(1)}, f32[512,256]{1,0:T(8,128)S(1)}, u32[]{:S(2)}, u32[]{:S(2)}) %collective-permute-start) | collective-permute-done | bytes 524320 | tf_op jit(solution)/shard_map/ppermute | solution.py:10
  50.8 11.7 %cholesky.374 = f32[128,128]{1,0:T(8,128)S(1)} custom-call(f32[128,128]{1,0:T(8,128)S(1)} %cholesky.586), custom_call_target="Cholesky" | custom-call | tf_op jit(solution)/shard_map/jit(cholesky)/cholesky | solution.py:35
  73.8 12.5 %cholesky.393 = f32[128,128]{1,0:T(8,128)S(1)} custom-call(f32[128,128]{1,0:T(8,128)} %cholesky.590), custom_call_target="Cholesky" | custom-call | tf_op jit(solution)/shard_map/jit(cholesky)/cholesky | solution.py:35
  87.0 10.8 %custom-call.47 = f32[1,128,128]{1,2,0:T(8,128)S(1)} custom-call(f32[1,128,128]{2,1,0:T(8,128)} %get-tuple-element.174), custom_call_target="InvertDiagBlocksLowerTriangular" | custom-call | tf_op jit(solution)/shard_map/jit(cholesky)/cholesky | solution.py:35
  98.5 11.7 %cholesky.414 = f32[128,128]{1,0:T(8,128)S(1)} custom-call(f32[128,128]{1,0:T(8,128)S(1)} %cholesky.595), custom_call_target="Cholesky" | custom-call | tf_op jit(solution)/shard_map/jit(cholesky)/cholesky | solution.py:35
  121.3 11.9 %cholesky.431 = f32[128,128]{1,0:T(8,128)S(1)} custom-call(f32[128,128]{1,0:T(8,128)S(1)} %convolution_subtract_fusion.30), custom_call_target="Cholesky" | custom-call | tf_op jit(solution)/shard_map/jit(cholesky)/cholesky | solution.py:35
  147.6 11.7 %cholesky.446 = f32[128,128]{1,0:T(8,128)S(1)} custom-call(f32[128,128]{1,0:T(8,128)S(1)} %cholesky.599), custom_call_target="Cholesky" | custom-call | tf_op jit(solution)/shard_map/jit(cholesky)/cholesky | solution.py:35
  160.2 40.5 %custom-call.50 = f32[4,128,128]{1,2,0:T(8,128)S(1)} custom-call(f32[4,128,128]{2,1,0:T(8,128)} %copy-done.49), custom_call_target="InvertDiagBlocksLowerTriangular" | custom-call | tf_op jit(solution)/shard_map/triangular_solve/custom-call.8 | solution.py:21
  212.0 11.7 %cholesky.465 = f32[128,128]{1,0:T(8,128)S(1)} custom-call(f32[128,128]{1,0:T(8,128)S(1)} %cholesky.603), custom_call_target="Cholesky" | custom-call | tf_op jit(solution)/shard_map/jit(cholesky)/cholesky | solution.py:35
  235.8 13.3 %cholesky.486 = f32[128,128]{1,0:T(8,128)} custom-call(f32[128,128]{1,0:T(8,128)} %cholesky.608), custom_call_target="Cholesky" | custom-call | tf_op jit(solution)/shard_map/jit(cholesky)/cholesky | solution.py:35
  250.6 11.3 %custom-call.53 = f32[1,128,128]{1,2,0:T(8,128)} custom-call(f32[1,128,128]{2,1,0:T(8,128)} %get-tuple-element.161), custom_call_target="InvertDiagBlocksLowerTriangular" | custom-call | tf_op jit(solution)/shard_map/jit(cholesky)/cholesky | solution.py:35
  263.3 11.7 %cholesky.503 = f32[128,128]{1,0:T(8,128)S(1)} custom-call(f32[128,128]{1,0:T(8,128)S(1)} %convolution_subtract_fusion.29), custom_call_target="Cholesky" | custom-call | tf_op jit(solution)/shard_map/jit(cholesky)/cholesky | solution.py:35
  287.8 39.5 %custom-call.55 = f32[4,128,128]{1,2,0:T(8,128)S(1)} custom-call(f32[4,128,128]{2,1,0:T(8,128)S(1)} %get-tuple-element.92), custom_call_target="InvertDiagBlocksLowerTriangular" | custom-call | tf_op jit(solution)/shard_map/triangular_solve/custom-call.8 | solution.py:21
  367.3 17.1 %collective-permute-done.2 = f32[512,256]{0,1:T(8,128)} collective-permute-done((f32[512,256]{0,1:T(8,128)}, f32[512,256]{0,1:T(8,128)}, u32[]{:S(2)}, u32[]{:S(2)}) %collective-permute-start.2) | collective-permute-done | bytes 524320 | tf_op jit(solution)/shard_map/ppermute | solution.py:10
  419.7 11.7 %cholesky.518 = f32[128,128]{1,0:T(8,128)S(1)} custom-call(f32[128,128]{1,0:T(8,128)S(1)} %cholesky.612), custom_call_target="Cholesky" | custom-call | tf_op jit(solution)/shard_map/jit(cholesky)/cholesky | solution.py:35
  432.1 10.4 %custom-call.56 = f32[1,128,128]{1,2,0:T(8,128)} custom-call(f32[1,128,128]{2,1,0:T(8,128)S(1)} %get-tuple-element.157), custom_call_target="InvertDiagBlocksLowerTriangular" | custom-call | tf_op jit(solution)/shard_map/jit(cholesky)/cholesky | solution.py:35
  447.3 13.6 %cholesky.537 = f32[128,128]{1,0:T(8,128)} custom-call(f32[128,128]{1,0:T(8,128)} %cholesky.616), custom_call_target="Cholesky" | custom-call | tf_op jit(solution)/shard_map/jit(cholesky)/cholesky | solution.py:35
  463.0 11.3 %custom-call.57 = f32[1,128,128]{1,2,0:T(8,128)} custom-call(f32[1,128,128]{2,1,0:T(8,128)} %get-tuple-element.154), custom_call_target="InvertDiagBlocksLowerTriangular" | custom-call | tf_op jit(solution)/shard_map/jit(cholesky)/cholesky | solution.py:35
  478.0 13.2 %cholesky.558 = f32[128,128]{1,0:T(8,128)} custom-call(f32[128,128]{1,0:T(8,128)} %cholesky.621), custom_call_target="Cholesky" | custom-call | tf_op jit(solution)/shard_map/jit(cholesky)/cholesky | solution.py:35
  493.4 11.3 %custom-call.58 = f32[1,128,128]{1,2,0:T(8,128)} custom-call(f32[1,128,128]{2,1,0:T(8,128)} %get-tuple-element.151), custom_call_target="InvertDiagBlocksLowerTriangular" | custom-call | tf_op jit(solution)/shard_map/jit(cholesky)/cholesky | solution.py:35
  507.5 13.3 %cholesky.575 = f32[128,128]{1,0:T(8,128)} custom-call(f32[128,128]{1,0:T(8,128)} %convolution_subtract_fusion.28), custom_call_target="Cholesky" | custom-call | tf_op jit(solution)/shard_map/jit(cholesky)/cholesky | solution.py:35
  527.3 10.5 %while.26 = (s32[]{:T(128)}, f32[512,512]{1,0:T(8,128)S(1)}, s32[4,2]{0,1:T(2,128)S(1)}, f32[4,128,128]{2,1,0:T(8,128)}, s32[]{:T(128)}) while((s32[]{:T(128)}, f32[512,512]{1,0:T(8,128)S(1)}, s32[4,2]{0,1:T(2,128)S(1)}, f32[4,128,128]{2,1,0:T(8,128)}, s32[]{:T(128)}) %tuple.141), condition=%wide.while_cond.1.clone.1, body=%wide.while_body.1.clone.1.sunk | while | flops 2 | bytes 132205 | solution.py:21
  537.8 40.8 %custom-call.60 = f32[4,128,128]{1,2,0:T(8,128)} custom-call(f32[4,128,128]{2,1,0:T(8,128)} %get-tuple-element.94), custom_call_target="InvertDiagBlocksLowerTriangular" | custom-call | tf_op jit(solution)/shard_map/triangular_solve/custom-call.8 | solution.py:21
  625.3 15.8 %collective-permute-done.4 = f32[512,256]{0,1:T(8,128)} collective-permute-done((f32[512,256]{0,1:T(8,128)S(1)}, f32[512,256]{0,1:T(8,128)}, u32[]{:S(2)}, u32[]{:S(2)}) %collective-permute-start.4) | collective-permute-done | bytes 524320 | tf_op jit(solution)/shard_map/ppermute | solution.py:10
  (379 shorter events, 278.2 us)
Async XLA Ops:
  7.2 322.8 %all-gather.9.cloned.1.call-start = ((), (), s32[]{:S(2)}) async-start(), calls=%async_computation.2 | async-start | bytes 1572864 | tf_op jit(solution)/shard_map/all_gather | solution.py:64
  8.3 20.1 %collective-permute-start = (f32[512,256]{1,0:T(8,128)S(1)}, f32[512,256]{1,0:T(8,128)S(1)}, u32[]{:S(2)}, u32[]{:S(2)}) collective-permute-start(f32[512,256]{1,0:T(8,128)S(1)} %slice.279), channel_id=1, source_target_pairs={{0,254},{2,0},{4,2},{6,4},{8,6},{10,8},{12,10},{14,12},{16,14},{18... | collective-permute-start | bytes 1572872 | tf_op jit(solution)/shard_map/ppermute | solution.py:10
  33.7 11.0 %all-to-all-start = ((f32[2,2048,256]{2,1,0:T(8,128)}), f32[2,2048,256]{2,1,0:T(8,128)}, u32[]{:S(2)}, u32[]{:S(2)}) async-start(f32[2,2048,256]{2,1,0:T(8,128)} %pad_maximum_fusion), calls=%async_computation | async-start | bytes 8388608 | tf_op jit(solution)/shard_map/all_to_all | solution.py:59
  39.4 292.4 %all-gather.7.cloned.1.call-start = ((), (), s32[]{:S(2)}) async-start(), calls=%async_computation.1 | async-start | bytes 6291456 | tf_op jit(solution)/shard_map/all_gather | solution.py:63
  41.3 373.0 %all-gather.13.cloned.1.call-start = ((), (), s32[]{:S(2)}) async-start(), calls=%async_computation.4 | async-start | bytes 1572864 | tf_op jit(solution)/shard_map/all_gather | solution.py:103
  50.8 21.7 %copy-start.22 = (f32[512,512]{1,0:T(8,128)S(1)}, f32[512,512]{1,0:T(8,128)}, u32[]{:S(2)}) copy-start(f32[512,512]{1,0:T(8,128)} %copy-done.21) | copy-start | bytes 3145732
  147.6 63.1 %copy-start.19 = (f32[512,512]{1,0:T(8,128)S(1)}, f32[512,512]{1,0:T(8,128)}, u32[]{:S(2)}) copy-start(f32[512,512]{1,0:T(8,128)} %copy-done.18) | copy-start | bytes 3145732
  327.3 25.8 %copy-start.13 = (f32[4,128,128]{1,2,0:T(8,128)}, f32[4,128,128]{1,2,0:T(8,128)S(1)}, u32[]{:S(2)}) copy-start(f32[4,128,128]{1,2,0:T(8,128)S(1)} %custom-call.55) | copy-start | bytes 786436
  348.4 11.3 %copy-start.7 = (f32[512,576]{0,1:T(8,128)}, f32[512,576]{0,1:T(8,128)S(1)}, u32[]{:S(2)}) copy-start(f32[512,576]{0,1:T(8,128)S(1)} %pad_maximum_fusion.2) | copy-start | bytes 3538948
  361.7 216.9 %all-gather.11.cloned.1.call-start = ((), (), s32[]{:S(2)}) async-start(), calls=%async_computation.3 | async-start | bytes 1572864 | tf_op jit(solution)/shard_map/all_gather | solution.py:105
  364.0 20.4 %collective-permute-start.2 = (f32[512,256]{0,1:T(8,128)}, f32[512,256]{0,1:T(8,128)}, u32[]{:S(2)}, u32[]{:S(2)}) collective-permute-start(f32[512,256]{0,1:T(8,128)} %get-tuple-element.145), channel_id=1, source_target_pairs={{0,2},{2,4},{4,6},{6,8},{8,10},{10,12},{12,14},{14,16},{16,18},{18... | collective-permute-start | bytes 1572872 | tf_op jit(solution)/shard_map/ppermute | solution.py:10
  367.2 215.6 %all-gather.15.cloned.1.call-start = ((), (), s32[]{:S(2)}) async-start(), calls=%async_computation.5 | async-start | bytes 1572864 | tf_op jit(solution)/shard_map/all_gather | solution.py:106
  388.4 15.1 %collective-permute-start.3 = (f32[512,256]{1,0:T(8,128)}, f32[512,256]{1,0:T(8,128)}, u32[]{:S(2)}, u32[]{:S(2)}) collective-permute-start(f32[512,256]{1,0:T(8,128)} %fusion), channel_id=1, source_target_pairs={{0,254},{2,0},{4,2},{6,4},{8,6},{10,8},{12,10},{14,12},{16,14},{18... | collective-permute-start | bytes 1572872 | tf_op jit(solution)/shard_map/ppermute | solution.py:10
  390.2 202.7 %collective-permute-start.8 = (f32[64,512]{1,0:T(8,128)}, f32[64,512]{1,0:T(8,128)}, u32[]{:S(2)}, u32[]{:S(2)}) collective-permute-start(f32[64,512]{1,0:T(8,128)} %param.16), channel_id=1, source_target_pairs={{0,254},{2,0},{4,2},{6,4},{8,6},{10,8},{12,10},{14,12},{16,14},{18... | collective-permute-start | bytes 393224 | tf_op jit(solution)/shard_map/ppermute | solution.py:10
  394.3 218.2 %collective-permute-start.6 = (f32[512,64]{0,1:T(8,128)}, f32[512,64]{0,1:T(8,128)}, u32[]{:S(2)}, u32[]{:S(2)}) collective-permute-start(f32[512,64]{0,1:T(8,128)} %pad_maximum_fusion.9), channel_id=1, source_target_pairs={{0,2},{2,4},{4,6},{6,8},{8,10},{10,12},{12,14},{14,16},{16,18},{18... | collective-permute-start | bytes 393224 | tf_op jit(solution)/shard_map/ppermute | solution.py:10
  396.4 220.0 %collective-permute-start.1 = (f32[512,256]{0,1:T(8,128)}, f32[512,256]{0,1:T(8,128)}, u32[]{:S(2)}, u32[]{:S(2)}) collective-permute-start(f32[512,256]{0,1:T(8,128)} %get-tuple-element.144), channel_id=1, source_target_pairs={{0,2},{2,4},{4,6},{6,8},{8,10},{10,12},{12,14},{14,16},{16,18},{18... | collective-permute-start | bytes 1572872 | tf_op jit(solution)/shard_map/ppermute | solution.py:10
  396.8 6.8 %copy-start.35 = (f32[64,2048]{1,0:T(8,128)S(1)}, f32[64,2048]{1,0:T(8,128)}, u32[]{:S(2)}) copy-start(f32[64,2048]{1,0:T(8,128)} %param.15) | copy-start | bytes 1572868
  403.5 216.2 %all-gather.17.cloned.1.call-start = ((), (), s32[]{:S(2)}) async-start(), calls=%async_computation.6 | async-start | bytes 1572864 | tf_op jit(solution)/shard_map/all_gather | solution.py:104
  537.8 40.8 %copy-start.4 = (f32[512,512]{1,0:T(8,128)}, f32[512,512]{1,0:T(8,128)S(1)}, u32[]{:S(2)}) copy-start(f32[512,512]{1,0:T(8,128)S(1)} %get-tuple-element.335) | copy-start | bytes 3145732
  592.8 5.9 copy-start.1
  610.1 12.1 %collective-permute-start.7 = (f32[512,64]{0,1:T(8,128)}, f32[512,64]{0,1:T(8,128)}, u32[]{:S(2)}, u32[]{:S(2)}) collective-permute-start(f32[512,64]{0,1:T(8,128)} %pad_maximum_fusion.7), channel_id=1, source_target_pairs={{0,2},{2,4},{4,6},{6,8},{8,10},{10,12},{12,14},{14,16},{16,18},{18... | collective-permute-start | bytes 393224 | tf_op jit(solution)/shard_map/ppermute | solution.py:10
  610.1 34.1 %collective-permute-start.5 = (f32[512,256]{0,1:T(8,128)}, f32[512,256]{0,1:T(8,128)}, u32[]{:S(2)}, u32[]{:S(2)}) collective-permute-start(f32[512,256]{0,1:T(8,128)} %get-tuple-element.142), channel_id=1, source_target_pairs={{0,2},{2,4},{4,6},{6,8},{8,10},{10,12},{12,14},{14,16},{16,18},{18... | collective-permute-start | bytes 1572872 | tf_op jit(solution)/shard_map/ppermute | solution.py:10
  610.1 31.0 %collective-permute-start.4 = (f32[512,256]{0,1:T(8,128)S(1)}, f32[512,256]{0,1:T(8,128)}, u32[]{:S(2)}, u32[]{:S(2)}) collective-permute-start(f32[512,256]{0,1:T(8,128)S(1)} %get-tuple-element.143), channel_id=1, source_target_pairs={{0,2},{2,4},{4,6},{6,8},{8,10},{10,12},{12,14},{14,16},{16,18},{18... | collective-permute-start | bytes 1572872 | tf_op jit(solution)/shard_map/ppermute | solution.py:10
  619.7 21.4 %copy-start.3 = (f32[512,512]{1,0:T(8,128)S(1)}, f32[512,512]{1,0:T(8,128)}, u32[]{:S(2)}) copy-start(f32[512,512]{1,0:T(8,128)} %all-gather.17.cloned.1.call-done) | copy-start | bytes 3145732
  (42 other events, 82.9 us)
Sparse Core Ops, SparseCore 0:
  29.3 14.0 all-gather.8
  45.1 19.7 all-gather.6
  361.8 13.2 all-gather.12
  377.3 15.6 all-gather.10
  403.7 12.2 all-gather.14
  418.1 15.7 all-gather.16
